TPU v7x, 256 devices: a whole 4x4x8 slice. The times are simulated.
256 devices in a mesh: row: 8 (over y, z_hi), col: 32 (over z_lo, x, core).
Axes of the slice: x: 4, y: 4, z: 8 (z_hi: 2, z_lo: 4; z = z_hi * 4 + z_lo), core: 2. Of those that a mesh axis runs over, the one named last changes fastest.
Arguments:
- embedding: bfloat16 [98304, 256], P(('col', 'row')), may hold values from -6 to 6
- weight: bfloat16 [256, 256], replicated, may hold values from -0.375 to 0.375
- grad_out: bfloat16 [98304, 256], P(('row', 'col')), may hold values from -6 to 6
- in_degree: int32 [98304], P(('row', 'col')), may hold values from 4 to 64
- out_degree: int32 [98304], P(('col', 'row')), may hold values from 4 to 64
- tile_edges: bfloat16 [8, 32, 192, 128, 128], P('row', 'col'), may hold values from 0 to 2, as said below
- tile_coords: int32 [8, 32, 192, 2], P('row', 'col'), may hold values from 0 to 95, as said below
- tile_count: int32 [8, 32], P('row', 'col'), may hold values from 48 to 192, as said below
Outputs:
- hidden: bfloat16 [98304, 256], P(('row', 'col'))
- grad_embedding: float32 [98304, 256], P(('col', 'row'))
- grad_weight: float32 [256, 256], replicated
Inputs may be any that keep to these rules, and one draw needn't show every extreme that they name: `tile_coords`: slots of one block name distinct tiles; entry 0 is a tile row below 96, entry 1 a tile column below 24. The live slots of a block are its first tile_count slots; some block has all 192 slots live. `tile_edges`: each entry is zero or a positive edge weight.
All inputs are finite; a program needn't handle non-finite values.
Results may differ from a plain program's by a relative error of at most 0.033.
Values may be sent and summed in bfloat16 or wider, within the bound.
No kernel may reach another device: no remote copies, remote signals or barrier semaphores. Data moves between devices by JAX's collectives and lax.ppermute only.
A program may use at most 128 MiB of HBM per device.

v0:
```python
import math
import jax
import jax.numpy as jnp
from jax import lax
from jax.sharding import PartitionSpec as P

decay_rate = 0.01


def tile_products(tile_set, source_ids, target_ids, alive, lookup, out_count, flipped):
    slots = tile_set.shape[0]
    block_count = max(1, slots // 64)
    per_block = slots // block_count

    def advance(running, number):
        first_slot = number * per_block
        block_tiles = lax.dynamic_slice_in_dim(tile_set, first_slot, per_block, 0)
        chosen = lax.dynamic_slice_in_dim(source_ids, first_slot, per_block, 0)
        picked = jnp.take(lookup, chosen, axis=0)
        if flipped:
            products = jnp.einsum(
                "tij,tif->tjf", block_tiles, picked, preferred_element_type=jnp.float32
            )
        else:
            products = jnp.einsum(
                "tij,tjf->tif", block_tiles, picked, preferred_element_type=jnp.float32
            )
        targets = lax.dynamic_slice_in_dim(target_ids, first_slot, per_block, 0)
        weights_alive = lax.dynamic_slice_in_dim(alive, first_slot, per_block, 0)
        products = products * weights_alive[:, None, None]
        running = running + jax.ops.segment_sum(products, targets, num_segments=out_count)
        return (running, None)

    initial = jnp.zeros((out_count, lookup.shape[1], lookup.shape[2]), jnp.float32)
    result, _ = lax.scan(advance, initial, jnp.arange(block_count))
    return result


def per_device(
    embedding, weight, grad_out, in_degree, out_degree, tile_edges, tile_coords, tile_count
):
    tile_set = tile_edges[0, 0]
    coords = tile_coords[0, 0]
    live_count = tile_count[0, 0]
    n_row = lax.axis_size("row")
    n_col = lax.axis_size("col")
    own_rows, width = embedding.shape
    edge_size = tile_set.shape[1]
    block_rows = own_rows * n_col
    block_cols = own_rows * n_row
    tile_rows = block_rows // edge_size
    tile_cols = block_cols // edge_size
    total_nodes = own_rows * n_row * n_col
    alive = (jnp.arange(tile_set.shape[0]) < live_count).astype(jnp.float32)
    scale_out = lax.rsqrt(out_degree.astype(jnp.float32))
    scaled = (scale_out[:, None] * embedding.astype(jnp.float32)).astype(jnp.bfloat16)
    source_block = lax.all_gather(scaled, "row", axis=0, tiled=True)
    forward_terms = tile_products(
        tile_set,
        coords[:, 1],
        coords[:, 0],
        alive,
        source_block.reshape(tile_cols, edge_size, width),
        tile_rows,
        False,
    )
    forward_terms = forward_terms.reshape(block_rows, width)
    summed = lax.psum_scatter(
        forward_terms.astype(jnp.bfloat16), "col", scatter_dimension=0, tiled=True
    ).astype(jnp.float32)
    scale_in = lax.rsqrt(in_degree.astype(jnp.float32))
    aggregate = (scale_in[:, None] * summed).astype(jnp.bfloat16)
    preact = jnp.dot(aggregate, weight, preferred_element_type=jnp.float32)
    gates = jax.nn.sigmoid(preact)
    hidden = (preact * gates).astype(jnp.bfloat16)
    delta_rows = (grad_out.astype(jnp.float32) * gates * (1.0 + preact * (1.0 - gates))).astype(
        jnp.bfloat16
    )
    local_weight = lax.dot_general(
        aggregate, delta_rows, (((0,), (0,)), ((), ())), preferred_element_type=jnp.float32
    )
    grad_weight = lax.psum(local_weight, ("row", "col")) / math.sqrt(total_nodes)
    projected = lax.dot_general(
        delta_rows, weight, (((1,), (1,)), ((), ())), preferred_element_type=jnp.float32
    )
    upstream = (scale_in[:, None] * projected).astype(jnp.bfloat16)
    upstream_block = lax.all_gather(upstream, "col", axis=0, tiled=True)
    backward_terms = tile_products(
        tile_set,
        coords[:, 0],
        coords[:, 1],
        alive,
        upstream_block.reshape(tile_rows, edge_size, width),
        tile_cols,
        True,
    )
    backward_terms = backward_terms.reshape(block_cols, width)
    source_total = lax.psum_scatter(
        backward_terms.astype(jnp.bfloat16), "row", scatter_dimension=0, tiled=True
    ).astype(jnp.float32)
    decay = decay_rate * jnp.sqrt(out_degree.astype(jnp.float32))
    grad_embedding = scale_out[:, None] * source_total + decay[:, None] * embedding.astype(
        jnp.float32
    )
    return (hidden, grad_embedding, grad_weight)


def solution(mesh):
    in_specs = (
        P(("col", "row"), None),
        P(),
        P(("row", "col"), None),
        P(("row", "col")),
        P(("col", "row")),
        P("row", "col", None, None, None),
        P("row", "col", None, None),
        P("row", "col"),
    )
    out_specs = (P(("row", "col"), None), P(("col", "row"), None), P())
    return jax.shard_map(
        per_device, mesh=mesh, in_specs=in_specs, out_specs=out_specs, check_vma=False
    )
```

profile of v0, /device:TPU:2, one launch (start us, length us, event | category | flops | bytes accessed | tf_op | source)
XLA Modules:
  0.0 763.7 jit_solution(9937921684894183327)
XLA Ops:
  7.2 1.3 sqrt_multiply_fusion
  8.5 0.5 copy-done.5
  9.1 1.7 fusion.19
  11.5 0.8 fusion.23
  12.3 71.1 %all-gather.3.cloned.1.call-done = bf16[3072,256]{1,0:T(8,128)(2,1)} async-done(((bf16[384,256]{1,0:T(8,128)(2,1)}), bf16[3072,256]{1,0:T(8,128)(2,1)}) %all-gather.3.cloned.1.call-update) | async-done | bytes 1572880 | tf_op jit(solution)/shard_map/all_gather | solution.py:57
  83.4 6.1 broadcast.23
  89.5 94.0 %while.20 = (s32[]{:T(128)}, f32[96,128,256]{2,1,0:T(8,128)}, s32[3]{0:T(128)S(1)}, s32[192]{0:T(256)S(1)}, bf16[192,128,128]{2,1,0:T(8,128)(2,1)}, /*index=5*/s...) while((s32[]{:T(128)}, f32[96,128,256]{2,1,0:T(8,128)}, ...), condition=%wide.region_2.3_spmd, body=%wide.region_0.2_spmd.sunk | while | flops 543163776 | bytes 48241472 | solution.py:35
  89.5 0.6 dynamic_slice.48
  90.7 0.1 compare_and_fusion.4
  90.8 2.8 gather_fusion
  93.6 0.1 dynamic_slice.50
  93.7 7.4 broadcast_multiply_fusion.5
  101.0 0.1 dynamic_slice.49
  101.1 19.7 %scatter_fusion = f32[96,128,256]{2,1,0:T(8,128)} fusion(f32[96,128,256]{2,1,0:T(8,128)} %get-tuple-element.258, s32[64]{0:T(128)S(1)} %dynamic_slice.49, f32[64,128,256]{2,1,0:T(8,128)} %broadcast_multiply_fusion.5), kind=kCustom, calls=%fused_computation.2.clone.1 | custom fusion | flops 2097152 | bytes 25166080 | tf_op jit(solution)/shard_map/while/body/eval_jaxpr/scatter-add | solution.py:31
  120.8 0.6 dynamic_slice.48
  122.1 0.1 compare_and_fusion.4
  122.1 2.8 gather_fusion
  124.9 0.1 dynamic_slice.50
  125.0 7.4 broadcast_multiply_fusion.5
  132.4 0.1 dynamic_slice.49
  132.4 19.8 %scatter_fusion = f32[96,128,256]{2,1,0:T(8,128)} fusion(f32[96,128,256]{2,1,0:T(8,128)} %get-tuple-element.258, s32[64]{0:T(128)S(1)} %dynamic_slice.49, f32[64,128,256]{2,1,0:T(8,128)} %broadcast_multiply_fusion.5), kind=kCustom, calls=%fused_computation.2.clone.1 | custom fusion | flops 2097152 | bytes 25166080 | tf_op jit(solution)/shard_map/while/body/eval_jaxpr/scatter-add | solution.py:31
  152.2 0.6 dynamic_slice.48
  153.5 0.1 compare_and_fusion.4
  153.6 2.8 gather_fusion
  156.3 0.1 dynamic_slice.50
  156.4 7.4 broadcast_multiply_fusion.5
  163.8 0.1 dynamic_slice.49
  163.8 19.6 %scatter_fusion = f32[96,128,256]{2,1,0:T(8,128)} fusion(f32[96,128,256]{2,1,0:T(8,128)} %get-tuple-element.258, s32[64]{0:T(128)S(1)} %dynamic_slice.49, f32[64,128,256]{2,1,0:T(8,128)} %broadcast_multiply_fusion.5), kind=kCustom, calls=%fused_computation.2.clone.1 | custom fusion | flops 2097152 | bytes 25166080 | tf_op jit(solution)/shard_map/while/body/eval_jaxpr/scatter-add | solution.py:31
  183.4 8.1 %convert_element_type.55 = bf16[96,128,256]{2,1,0:T(8,128)(2,1)} convert(f32[96,128,256]{2,1,0:T(8,128)} %get-tuple-element.87) | non-fusion elementwise | flops 3145728 | bytes 18874368 | tf_op jit(solution)/shard_map/convert_element_type | solution.py:69
  191.6 0.6 copy-done.8
  192.2 143.5 %reduce-scatter.3.cloned.1.call-done = bf16[384,256]{1,0:T(8,128)(2,1)} async-done(((bf16[12288,256]{1,0:T(8,128)(2,1)}), bf16[384,256]{1,0:T(8,128)(2,1)}) %reduce-scatter.3.cloned.1.call-update) | async-done | bytes 196624 | tf_op jit(solution)/shard_map/reduce_scatter | solution.py:68
  335.7 2.0 multiply_convert_fusion
  337.7 0.9 fusion.18
  338.8 8.7 %copy.11 = bf16[1,1,192,128,128]{3,4,2,1,0:T(8,128)(2,1)} copy(bf16[1,1,192,128,128]{4,3,2,1,0:T(8,128)(2,1)} %bitcast.24) | data formatting | bytes 12582912 | tf_op args[5]
  347.5 1.1 fusion.21
  348.6 58.1 %all-gather.5.cloned.1.call-done = bf16[12288,256]{1,0:T(8,128)(2,1)} async-done(((bf16[384,256]{1,0:T(8,128)(2,1)}), bf16[12288,256]{1,0:T(8,128)(2,1)}) %all-gather.5.cloned.1.call-update) | async-done | bytes 6291472 | tf_op jit(solution)/shard_map/all_gather | solution.py:87
  406.7 0.3 broadcast.25
  407.0 80.9 %while.21 = (s32[]{:T(128)}, f32[24,128,256]{2,1,0:T(8,128)S(1)}, s32[3]{0:T(128)S(1)}, s32[192]{0:T(256)S(1)}, bf16[192,128,128]{1,2,0:T(8,128)(2,1)}, /*index=...) while((s32[]{:T(128)}, f32[24,128,256]{2,1,0:T(8,128)S(1)}, ...), condition=%wide.region_6.7_spmd, body=%wide.region_4.6_spmd.sunk | while | flops 543163776 | bytes 48241472 | solution.py:35
  407.0 0.6 dynamic_slice.52
  408.3 0.1 compare_and_fusion.5
  408.4 5.6 gather_fusion.1
  413.9 0.1 dynamic_slice.54
  414.0 7.4 broadcast_multiply_fusion.6
  421.4 0.1 dynamic_slice.53
  421.5 12.5 %scatter_fusion.1 = f32[24,128,256]{2,1,0:T(8,128)S(1)} fusion(f32[24,128,256]{2,1,0:T(8,128)S(1)} %get-tuple-element.294, s32[64]{0:T(128)S(1)} %dynamic_slice.53, f32[64,128,256]{2,1,0:T(8,128)} %broadcast_multiply_fusion.6), kind=kCustom, calls=%fused_computation.3.clone.1 | custom fusion | flops 2097152 | bytes 25166080 | tf_op jit(solution)/shard_map/while/body/eval_jaxpr/scatter-add | solution.py:31
  433.9 0.6 dynamic_slice.52
  435.2 0.1 compare_and_fusion.5
  435.3 5.6 gather_fusion.1
  440.9 0.1 dynamic_slice.54
  441.0 7.4 broadcast_multiply_fusion.6
  448.4 0.1 dynamic_slice.53
  448.4 12.5 %scatter_fusion.1 = f32[24,128,256]{2,1,0:T(8,128)S(1)} fusion(f32[24,128,256]{2,1,0:T(8,128)S(1)} %get-tuple-element.294, s32[64]{0:T(128)S(1)} %dynamic_slice.53, f32[64,128,256]{2,1,0:T(8,128)} %broadcast_multiply_fusion.6), kind=kCustom, calls=%fused_computation.3.clone.1 | custom fusion | flops 2097152 | bytes 25166080 | tf_op jit(solution)/shard_map/while/body/eval_jaxpr/scatter-add | solution.py:31
  460.9 0.6 dynamic_slice.52
  462.2 0.1 compare_and_fusion.5
  462.3 5.6 gather_fusion.1
  467.9 0.1 dynamic_slice.54
  468.0 7.4 broadcast_multiply_fusion.6
  475.4 0.1 dynamic_slice.53
  475.4 12.5 %scatter_fusion.1 = f32[24,128,256]{2,1,0:T(8,128)S(1)} fusion(f32[24,128,256]{2,1,0:T(8,128)S(1)} %get-tuple-element.294, s32[64]{0:T(128)S(1)} %dynamic_slice.53, f32[64,128,256]{2,1,0:T(8,128)} %broadcast_multiply_fusion.6), kind=kCustom, calls=%fused_computation.3.clone.1 | custom fusion | flops 2097152 | bytes 25166080 | tf_op jit(solution)/shard_map/while/body/eval_jaxpr/scatter-add | solution.py:31
  488.0 1.4 convert_element_type.63
  489.4 172.9 %all-reduce.2.cloned.1.call-done = f32[256,256]{1,0:T(8,128)} async-done(((f32[256,256]{1,0:T(8,128)}), f32[256,256]{1,0:T(8,128)}) %all-reduce.2.cloned.1.call-update) | async-done | bytes 262160 | tf_op jit(solution)/shard_map/psum | solution.py:82
  662.3 1.7 broadcast_multiply_fusion.2
  664.0 91.3 %reduce-scatter.5.cloned.1.call-done = bf16[384,256]{1,0:T(8,128)(2,1)} async-done(((bf16[3072,256]{1,0:T(8,128)(2,1)}), bf16[384,256]{1,0:T(8,128)(2,1)}) %reduce-scatter.5.cloned.1.call-update) | async-done | bytes 196624 | tf_op jit(solution)/shard_map/reduce_scatter | solution.py:98
  755.3 1.8 fusion.20
  (38 shorter events, 0.4 us)
Async XLA Ops:
  7.2 328.6 %copy-start = (bf16[256,256]{1,0:T(8,128)(2,1)S(1)}, bf16[256,256]{1,0:T(8,128)(2,1)}, u32[]{:S(2)}) copy-start(bf16[256,256]{1,0:T(8,128)(2,1)} %param.13) | copy-start | bytes 393220
  7.2 76.2 %all-gather.3.cloned.1.call-start = ((), (), s32[]{:S(2)}) async-start(), calls=%async_computation.2 | async-start | bytes 1769472 | tf_op jit(solution)/shard_map/all_gather | solution.py:57
  8.5 0.5 copy-start.5
  10.8 324.9 %reduce-scatter.3.cloned.1.call-start = ((), (), s32[]{:S(2)}) async-start(), calls=%async_computation.3 | async-start | bytes 6488064 | tf_op jit(solution)/shard_map/reduce_scatter | solution.py:68
  83.4 6.1 copy-start.2
  191.6 0.7 copy-start.8
  191.6 144.2 %copy-start.9 = (bf16[384,256]{1,0:T(8,128)(2,1)S(1)}, bf16[384,256]{1,0:T(8,128)(2,1)}, u32[]{:S(2)}) copy-start(bf16[384,256]{1,0:T(8,128)(2,1)} %param.14) | copy-start | bytes 589828
  191.6 215.1 %all-gather.5.cloned.1.call-start = ((), (), s32[]{:S(2)}) async-start(), calls=%async_computation.4 | async-start | bytes 6488064 | tf_op jit(solution)/shard_map/all_gather | solution.py:87
  338.7 8.8 %copy-start.4 = (bf16[384,256]{1,0:T(8,128)(2,1)S(1)}, bf16[384,256]{1,0:T(8,128)(2,1)}, u32[]{:S(2)}) copy-start(bf16[384,256]{1,0:T(8,128)(2,1)} %reduce-scatter.3.cloned.1.call-done) | copy-start | bytes 589828
  338.7 323.6 %all-reduce.2.cloned.1.call-start = ((), (), s32[]{:S(2)}) async-start(), calls=%async_computation.6 | async-start | bytes 524288 | tf_op jit(solution)/shard_map/psum | solution.py:82
  348.6 406.7 %reduce-scatter.5.cloned.1.call-start = ((), (), s32[]{:S(2)}) async-start(), calls=%async_computation.5 | async-start | bytes 1769472 | tf_op jit(solution)/shard_map/reduce_scatter | solution.py:98
  487.9 267.4 %copy-start.3 = (bf16[384,256]{1,0:T(8,128)(2,1)S(1)}, bf16[384,256]{1,0:T(8,128)(2,1)}, u32[]{:S(2)}) copy-start(bf16[384,256]{1,0:T(8,128)(2,1)} %param.12) | copy-start | bytes 589828
  487.9 267.4 %copy-start.6 = (f32[384]{0:T(512)S(1)}, f32[384]{0:T(512)}, u32[]{:S(2)}) copy-start(f32[384]{0:T(512)} %copy-done.5) | copy-start | bytes 4612
  487.9 267.3 %copy-start.7 = (f32[384]{0:T(512)S(1)}, f32[384]{0:T(512)}, u32[]{:S(2)}) copy-start(f32[384]{0:T(512)} %get-tuple-element.135) | copy-start | bytes 4612
  487.9 269.2 %copy-start.1 = (bf16[256,256]{1,0:T(8,128)(2,1)S(1)}, bf16[256,256]{1,0:T(8,128)(2,1)}, u32[]{:S(2)}) copy-start(bf16[256,256]{1,0:T(8,128)(2,1)} %param.13) | copy-start | bytes 393220
Sparse Core Ops, SparseCore 0:
  11.2 72.1 all-gather.2
  191.7 143.9 reduce-scatter.2
  338.8 67.8 all-gather.4
  412.6 249.7 all-reduce.1
  666.2 89.0 reduce-scatter.4
where the time goes:
time: 765 us; the launch traced here: 764 us
  waiting for transfers between devices  537 us (70%)
  other arithmetic  113 us (15%)
  matrix products  48.2 us (6%)
  local copies, waits for them, and re-layouts  46.6 us (6%)
  between operations  14.5 us (2%)
    psum x1, waiting for transfers between devices, per_device(): lax.psum(local_weight, ('row', 'col')) / math.sqrt(total_nodes)  173 us
    reduce_scatter x1, waiting for transfers between devices, per_device(): lax.psum_scatter(forward_terms.astype(jnp.bfloat16), 'col', scatter_dimen...  143 us
    scatter-add x6, other arithmetic, advance(): jax.ops.segment_sum(products, targets, num_segments=out_count)  96.5 us
    reduce_scatter x1, waiting for transfers between devices, per_device(): lax.psum_scatter(backward_terms.astype(jnp.bfloat16), 'row', scatter_dime...  91.3 us
    all_gather x1, waiting for transfers between devices, per_device(): source_block = lax.all_gather(scaled, 'row', axis=0, tiled=True)  71.1 us
    all_gather x1, waiting for transfers between devices, per_device(): upstream_block = lax.all_gather(upstream, 'col', axis=0, tiled=True)  58.1 us
    gather x6, local copies, waits for them, and re-layouts, advance(): picked = jnp.take(lookup, chosen, axis=0)  25.2 us
    dot_general x3, matrix products, advance(): jnp.einsum('tij,tif->tjf', block_tiles, picked, preferred_element_type=jn...  22.2 us
  transfers between devices with their start and end apart: 5, of which 5 were waited for; matrix products, arithmetic and copies ran while one was open for 12% of the time, Pallas kernels for 0%

commit v1 on v0

--- a/solution.py
+++ b/solution.py
@@ -79,7 +79,9 @@
     local_weight = lax.dot_general(
         aggregate, delta_rows, (((0,), (0,)), ((), ())), preferred_element_type=jnp.float32
     )
-    grad_weight = lax.psum(local_weight, ("row", "col")) / math.sqrt(total_nodes)
+    grad_weight = jnp.sum(lax.all_gather(local_weight, ("row", "col")), axis=0) / math.sqrt(
+        total_nodes
+    )
     projected = lax.dot_general(
         delta_rows, weight, (((1,), (1,)), ((), ())), preferred_element_type=jnp.float32
     )

time: 765 us -> 823 us (1.076)
  waiting for transfers between devices: 537 us -> 573 us
  other arithmetic: 113 us -> 133 us
    all_gather x0 -> x1, waiting for transfers between devices: none -> 211 us  [per_device(): lax.all_gather(local_weight, ('row', 'col'))]
    psum x1 -> x0, waiting for transfers between devices: 173 us -> none  [per_device(): lax.psum(local_weight, ('row', 'col')) / math.sqrt(total_nodes)]
    reduce_sum x0 -> x1, other arithmetic: none -> 21.1 us  [per_device(): jnp.sum(lax.all_gather(local_weight, ('row', 'col')), axis=0)]
  transfers between devices with their start and end apart: 5 -> 5, of which waited for: 5 -> 5; matrix products, arithmetic and copies ran while one was open for 12% -> 2% of each run, Pallas kernels for 0% -> 0%
where the time goes in v1:
time: 823 us; the launch traced here: 821 us
  waiting for transfers between devices  573 us (70%)
  other arithmetic  133 us (16%)
  matrix products  49.2 us (6%)
  local copies, waits for them, and re-layouts  47.3 us (6%)
  between operations  14.5 us (2%)
    all_gather x1, waiting for transfers between devices, per_device(): lax.all_gather(local_weight, ('row', 'col'))  211 us
    reduce_scatter x1, waiting for transfers between devices, per_device(): lax.psum_scatter(forward_terms.astype(jnp.bfloat16), 'col', scatter_dimen...  143 us
    scatter-add x6, other arithmetic, advance(): jax.ops.segment_sum(products, targets, num_segments=out_count)  96.4 us
    reduce_scatter x1, waiting for transfers between devices, per_device(): lax.psum_scatter(backward_terms.astype(jnp.bfloat16), 'row', scatter_dime...  87.7 us
    all_gather x1, waiting for transfers between devices, per_device(): source_block = lax.all_gather(scaled, 'row', axis=0, tiled=True)  71 us
    all_gather x1, waiting for transfers between devices, per_device(): upstream_block = lax.all_gather(upstream, 'col', axis=0, tiled=True)  59.9 us
    gather x6, local copies, waits for them, and re-layouts, advance(): picked = jnp.take(lookup, chosen, axis=0)  25.1 us
    dot_general x3, matrix products, advance(): jnp.einsum('tij,tif->tjf', block_tiles, picked, preferred_element_type=jn...  22.1 us
  transfers between devices with their start and end apart: 5, of which 5 were waited for; matrix products, arithmetic and copies ran while one was open for 2% of the time, Pallas kernels for 0%

profile of v1, /device:TPU:2, one launch (start us, length us, event | category | flops | bytes accessed | tf_op | source)
XLA Modules:
  0.0 820.9 jit_solution(7401669873284857490)
XLA Ops:
  7.2 1.3 sqrt_multiply_fusion
  8.5 0.6 copy-done.5
  9.1 1.7 fusion.19
  11.6 0.8 fusion.23
  12.3 71.0 %all-gather.5.cloned.1.call-done = bf16[3072,256]{1,0:T(8,128)(2,1)} async-done(((bf16[384,256]{1,0:T(8,128)(2,1)}), bf16[3072,256]{1,0:T(8,128)(2,1)}) %all-gather.5.cloned.1.call-update) | async-done | bytes 1572880 | tf_op jit(solution)/shard_map/all_gather | solution.py:57
  83.4 6.1 broadcast.23
  89.5 94.0 %while.20 = (s32[]{:T(128)}, f32[96,128,256]{2,1,0:T(8,128)}, s32[3]{0:T(128)S(1)}, s32[192]{0:T(256)S(1)}, bf16[192,128,128]{2,1,0:T(8,128)(2,1)}, /*index=5*/s...) while((s32[]{:T(128)}, f32[96,128,256]{2,1,0:T(8,128)}, ...), condition=%wide.region_2.3_spmd, body=%wide.region_0.2_spmd.sunk | while | flops 543163776 | bytes 48241480 | solution.py:35
  89.5 0.6 dynamic_slice.48
  90.7 0.1 dynamic_slice.50
  90.8 0.1 dynamic_slice.49
  90.9 0.1 compare_and_fusion.4
  90.9 2.8 gather_fusion
  93.7 7.4 broadcast_multiply_fusion.5
  101.1 19.7 %scatter_fusion = f32[96,128,256]{2,1,0:T(8,128)} fusion(f32[96,128,256]{2,1,0:T(8,128)} %get-tuple-element.258, s32[64]{0:T(128)S(1)} %dynamic_slice.49, f32[64,128,256]{2,1,0:T(8,128)} %broadcast_multiply_fusion.5), kind=kCustom, calls=%fused_computation.2.clone.1 | custom fusion | flops 2097152 | bytes 25166080 | tf_op jit(solution)/shard_map/while/body/eval_jaxpr/scatter-add | solution.py:31
  120.8 0.6 dynamic_slice.48
  122.1 0.1 dynamic_slice.50
  122.1 0.1 dynamic_slice.49
  122.2 0.1 compare_and_fusion.4
  122.3 2.8 gather_fusion
  125.1 7.4 broadcast_multiply_fusion.5
  132.4 19.8 %scatter_fusion = f32[96,128,256]{2,1,0:T(8,128)} fusion(f32[96,128,256]{2,1,0:T(8,128)} %get-tuple-element.258, s32[64]{0:T(128)S(1)} %dynamic_slice.49, f32[64,128,256]{2,1,0:T(8,128)} %broadcast_multiply_fusion.5), kind=kCustom, calls=%fused_computation.2.clone.1 | custom fusion | flops 2097152 | bytes 25166080 | tf_op jit(solution)/shard_map/while/body/eval_jaxpr/scatter-add | solution.py:31
  152.2 0.6 dynamic_slice.48
  153.5 0.1 dynamic_slice.50
  153.5 0.1 dynamic_slice.49
  153.6 0.1 compare_and_fusion.4
  153.7 2.8 gather_fusion
  156.5 7.4 broadcast_multiply_fusion.5
  163.9 19.6 %scatter_fusion = f32[96,128,256]{2,1,0:T(8,128)} fusion(f32[96,128,256]{2,1,0:T(8,128)} %get-tuple-element.258, s32[64]{0:T(128)S(1)} %dynamic_slice.49, f32[64,128,256]{2,1,0:T(8,128)} %broadcast_multiply_fusion.5), kind=kCustom, calls=%fused_computation.2.clone.1 | custom fusion | flops 2097152 | bytes 25166080 | tf_op jit(solution)/shard_map/while/body/eval_jaxpr/scatter-add | solution.py:31
  183.4 8.1 convert_element_type.55
  191.6 0.6 copy-done.8
  192.3 143.1 %reduce-scatter.3.cloned.1.call-done = bf16[384,256]{1,0:T(8,128)(2,1)} async-done(((bf16[12288,256]{1,0:T(8,128)(2,1)}), bf16[384,256]{1,0:T(8,128)(2,1)}) %reduce-scatter.3.cloned.1.call-update) | async-done | bytes 196624 | tf_op jit(solution)/shard_map/reduce_scatter | solution.py:68
  335.4 2.0 multiply_convert_fusion
  337.4 0.7 copy-done.4
  338.0 0.9 fusion.18
  339.0 8.7 %copy.11 = bf16[1,1,192,128,128]{3,4,2,1,0:T(8,128)(2,1)} copy(bf16[1,1,192,128,128]{4,3,2,1,0:T(8,128)(2,1)} %bitcast.25) | data formatting | bytes 12582912 | tf_op args[5]
  347.7 59.9 %all-gather.7.cloned.1.call-done = bf16[12288,256]{1,0:T(8,128)(2,1)} async-done(((bf16[384,256]{1,0:T(8,128)(2,1)}), bf16[12288,256]{1,0:T(8,128)(2,1)}) %all-gather.7.cloned.1.call-update) | async-done | bytes 6291472 | tf_op jit(solution)/shard_map/all_gather | solution.py:89
  407.6 0.3 broadcast.25
  408.0 80.7 %while.21 = (s32[]{:T(128)}, f32[24,128,256]{2,1,0:T(8,128)S(1)}, s32[3]{0:T(128)S(1)}, s32[192]{0:T(256)S(1)}, bf16[192,128,128]{1,2,0:T(8,128)(2,1)}, /*index=...) while((s32[]{:T(128)}, f32[24,128,256]{2,1,0:T(8,128)S(1)}, ...), condition=%wide.region_6.7_spmd, body=%wide.region_4.6_spmd.sunk | while | flops 543163776 | bytes 48241480 | solution.py:35
  408.0 0.6 dynamic_slice.52
  409.2 0.1 dynamic_slice.54
  409.4 0.1 compare_and_fusion.5
  409.5 5.6 gather_fusion.1
  415.0 7.4 broadcast_multiply_fusion.6
  422.4 12.4 %scatter_fusion.1 = f32[24,128,256]{2,1,0:T(8,128)S(1)} fusion(f32[24,128,256]{2,1,0:T(8,128)S(1)} %get-tuple-element.294, s32[64]{0:T(128)S(1)} %dynamic_slice.53, f32[64,128,256]{2,1,0:T(8,128)} %broadcast_multiply_fusion.6), kind=kCustom, calls=%fused_computation.3.clone.1 | custom fusion | flops 2097152 | bytes 25166080 | tf_op jit(solution)/shard_map/while/body/eval_jaxpr/scatter-add | solution.py:31
  434.9 0.6 dynamic_slice.52
  436.1 0.1 dynamic_slice.54
  436.3 0.1 compare_and_fusion.5
  436.4 5.6 gather_fusion.1
  441.9 7.4 broadcast_multiply_fusion.6
  449.3 12.4 %scatter_fusion.1 = f32[24,128,256]{2,1,0:T(8,128)S(1)} fusion(f32[24,128,256]{2,1,0:T(8,128)S(1)} %get-tuple-element.294, s32[64]{0:T(128)S(1)} %dynamic_slice.53, f32[64,128,256]{2,1,0:T(8,128)} %broadcast_multiply_fusion.6), kind=kCustom, calls=%fused_computation.3.clone.1 | custom fusion | flops 2097152 | bytes 25166080 | tf_op jit(solution)/shard_map/while/body/eval_jaxpr/scatter-add | solution.py:31
  461.8 0.6 dynamic_slice.52
  463.0 0.1 dynamic_slice.54
  463.1 0.1 dynamic_slice.53
  463.2 0.1 compare_and_fusion.5
  463.3 5.6 gather_fusion.1
  468.8 7.4 broadcast_multiply_fusion.6
  476.2 12.4 %scatter_fusion.1 = f32[24,128,256]{2,1,0:T(8,128)S(1)} fusion(f32[24,128,256]{2,1,0:T(8,128)S(1)} %get-tuple-element.294, s32[64]{0:T(128)S(1)} %dynamic_slice.53, f32[64,128,256]{2,1,0:T(8,128)} %broadcast_multiply_fusion.6), kind=kCustom, calls=%fused_computation.3.clone.1 | custom fusion | flops 2097152 | bytes 25166080 | tf_op jit(solution)/shard_map/while/body/eval_jaxpr/scatter-add | solution.py:31
  488.7 1.4 convert_element_type.63
  490.2 2.1 fusion.21
  492.3 87.7 %reduce-scatter.5.cloned.1.call-done = bf16[384,256]{1,0:T(8,128)(2,1)} async-done(((bf16[3072,256]{1,0:T(8,128)(2,1)}), bf16[384,256]{1,0:T(8,128)(2,1)}) %reduce-scatter.5.cloned.1.call-update) | async-done | bytes 196624 | tf_op jit(solution)/shard_map/reduce_scatter | solution.py:100
  580.0 1.8 fusion.20
  581.9 210.7 %all-gather.9.cloned.1.call-done = f32[65536,256]{1,0:T(8,128)} async-done(((f32[256,256]{1,0:T(8,128)}), f32[65536,256]{1,0:T(8,128)}) %all-gather.9.cloned.1.call-update) | async-done | bytes 67108880 | tf_op jit(solution)/shard_map/all_gather | solution.py:82
  792.6 21.1 %reduce_sum.9 = f32[256,256]{1,0:T(8,128)S(1)} reduce(f32[256,256,256]{2,1,0:T(8,128)} %bitcast.12, f32[]{:T(128)} %constant.63.clone.1), dimensions={0}, to_apply=%region_8.9 | reduce | flops 16711680 | bytes 67371008 | tf_op jit(solution)/shard_map/reduce_sum | solution.py:82
  813.6 0.7 broadcast_multiply_fusion.2
  (39 shorter events, 0.5 us)
Async XLA Ops:
  7.2 328.2 %copy-start = (bf16[256,256]{1,0:T(8,128)(2,1)S(1)}, bf16[256,256]{1,0:T(8,128)(2,1)}, u32[]{:S(2)}) copy-start(bf16[256,256]{1,0:T(8,128)(2,1)} %param.13) | copy-start | bytes 393220
  7.2 76.2 %all-gather.5.cloned.1.call-start = ((), (), s32[]{:S(2)}) async-start(), calls=%async_computation.2 | async-start | bytes 1769472 | tf_op jit(solution)/shard_map/all_gather | solution.py:57
  8.5 0.6 copy-start.5
  10.9 324.5 %reduce-scatter.3.cloned.1.call-start = ((), (), s32[]{:S(2)}) async-start(), calls=%async_computation.3 | async-start | bytes 6488064 | tf_op jit(solution)/shard_map/reduce_scatter | solution.py:68
  83.4 6.1 copy-start.2
  191.6 0.7 copy-start.8
  191.6 143.8 %copy-start.9 = (bf16[384,256]{1,0:T(8,128)(2,1)S(1)}, bf16[384,256]{1,0:T(8,128)(2,1)}, u32[]{:S(2)}) copy-start(bf16[384,256]{1,0:T(8,128)(2,1)} %param.14) | copy-start | bytes 589828
  191.6 216.0 %all-gather.7.cloned.1.call-start = ((), (), s32[]{:S(2)}) async-start(), calls=%async_computation.4 | async-start | bytes 6488064 | tf_op jit(solution)/shard_map/all_gather | solution.py:89
  337.4 0.7 copy-start.4
  339.0 241.0 %reduce-scatter.5.cloned.1.call-start = ((), (), s32[]{:S(2)}) async-start(), calls=%async_computation.5 | async-start | bytes 1769472 | tf_op jit(solution)/shard_map/reduce_scatter | solution.py:100
  488.7 91.3 %copy-start.3 = (bf16[384,256]{1,0:T(8,128)(2,1)S(1)}, bf16[384,256]{1,0:T(8,128)(2,1)}, u32[]{:S(2)}) copy-start(bf16[384,256]{1,0:T(8,128)(2,1)} %param.12) | copy-start | bytes 589828
  488.7 91.3 %copy-start.6 = (f32[384]{0:T(512)S(1)}, f32[384]{0:T(512)}, u32[]{:S(2)}) copy-start(f32[384]{0:T(512)} %copy-done.5) | copy-start | bytes 4612
  488.7 91.3 %copy-start.7 = (f32[384]{0:T(512)S(1)}, f32[384]{0:T(512)}, u32[]{:S(2)}) copy-start(f32[384]{0:T(512)} %get-tuple-element.135) | copy-start | bytes 4612
  490.2 302.4 %all-gather.9.cloned.1.call-start = ((), (), s32[]{:S(2)}) async-start(), calls=%async_computation.6 | async-start | bytes 67371008 | tf_op jit(solution)/shard_map/all_gather | solution.py:82
  792.6 21.8 %copy-start.1 = (bf16[256,256]{1,0:T(8,128)(2,1)S(1)}, bf16[256,256]{1,0:T(8,128)(2,1)}, u32[]{:S(2)}) copy-start(bf16[256,256]{1,0:T(8,128)(2,1)} %param.13) | copy-start | bytes 393220
Sparse Core Ops, SparseCore 0:
  11.2 72.1 all-gather.4
  191.7 143.5 reduce-scatter.2
  339.1 68.4 all-gather.6
  490.3 89.6 reduce-scatter.4
  584.0 208.4 all-gather.8
